TPU v7x, 32 devices: a whole 2x2x4 slice. The times are simulated.
32 devices in a mesh: ctx: 8 (over y, x, core), mp: 4 (over z).
Axes of the slice: x: 2, y: 2, z: 4, core: 2. Of those that a mesh axis runs over, the one named last changes fastest.
Arguments:
- queries: bfloat16 [128, 6144], P('ctx', 'mp'), may hold values from -9 to 9
- cache_keys: bfloat16 [8, 4096, 128], P('mp', 'ctx'), may hold values from -9 to 9, as said below
- cache_values: bfloat16 [8, 4096, 128], P('mp', 'ctx'), may hold values from -6 to 6, as said below
- new_keys: bfloat16 [8, 128, 128], P('mp', 'ctx'), may hold values from -6 to 6, as said below
- new_values: bfloat16 [8, 128, 128], P('mp', 'ctx'), may hold values from -6 to 6, as said below
- out_proj: bfloat16 [6144, 6144], P('mp', 'ctx'), may hold values from -3 to 3
- residual: bfloat16 [128, 6144], P('mp', 'ctx'), may hold values from -24 to 24
- norm_gain: bfloat16 [6144], replicated, may hold values from 0.5 to 1.5
- gate_proj: bfloat16 [8, 6144, 8192], P('ctx', None, 'mp'), may hold values from -0.078125 to 0.078125
- up_proj: bfloat16 [8, 6144, 8192], P('ctx', None, 'mp'), may hold values from -0.078125 to 0.078125
- down_proj: bfloat16 [8, 8192, 6144], P('ctx', 'mp'), may hold values from -0.09375 to 0.09375
- expert_ids: int32 [128, 2], replicated, may hold values from 0 to 7, all different within a row; in each aligned block of 128 rows (0 to 127, 128 to 255, ...) at most 64 rows name the same one
- route_logits: float32 [128, 2], replicated, may hold values from -6 to 6
Outputs:
- layer_out: bfloat16 [128, 6144], P('mp', 'ctx')
Inputs may be any that keep to these rules, and one draw needn't show every extreme that they name: `expert_ids`: each row names 2 different experts; at most 64 rows name one expert, a bound that some block reaches. `cache_keys`: slot s holds key head s * 1; slots of one key head are equal. `cache_values`: slot s holds value head s * 1; slots of one head are equal. `new_keys`: slot s holds key head s * 1; slots of one key head are equal. `new_values`: slot s holds value head s * 1; slots of one head are equal.
All inputs are finite; a program needn't handle non-finite values.
Results may differ from a plain program's by a relative error of at most 0.024.
Values may be sent and summed in bfloat16 or wider, within the bound.
No kernel may reach another device: no remote copies, remote signals or barrier semaphores. Data moves between devices by JAX's collectives and lax.ppermute only.
A program may use at most 128 MiB of HBM per device.

v0:
```python
import math
import jax
import jax.numpy as jnp
from jax import lax
from jax.sharding import PartitionSpec as P

D = 6144
EXPERTS = 8
TOP = 2
neg_big = -1e30
norm_eps = 1e-05


def route_slots(expert_ids):
    flat = expert_ids.reshape(-1)
    onehot = (flat[:, None] == jnp.arange(EXPERTS, dtype=jnp.int32)[None, :]).astype(jnp.int32)
    before = jnp.cumsum(onehot, axis=0, dtype=jnp.int32) - onehot
    return jnp.sum(before * onehot, axis=1, dtype=jnp.int32).reshape(expert_ids.shape)


def softmax_pieces(query_block, keys_local, values_local, allowed, scale):
    scores = (
        jnp.einsum("srd,skd->srk", query_block, keys_local, preferred_element_type=jnp.float32)
        * scale
    )
    scores = jnp.where(allowed[None, :, :], scores, neg_big)
    highest = jnp.max(scores, axis=2)
    expo = jnp.exp(scores - highest[:, :, None])
    denom = jnp.sum(expo, axis=2)
    summed = jnp.einsum(
        "srk,skd->srd", expo.astype(jnp.bfloat16), values_local, preferred_element_type=jnp.float32
    )
    return (highest, denom, summed)


def join_softmax(former, latter):
    highest = jnp.maximum(former[0], latter[0])
    right = jnp.exp(latter[0] - highest)
    denom = latter[1] * right
    summed = latter[2] * right[:, :, None]
    return (highest, denom, summed)


def on_device(
    queries,
    cache_keys,
    cache_values,
    new_keys,
    new_values,
    out_proj,
    residual,
    norm_gain,
    gate_proj,
    up_proj,
    down_proj,
    expert_ids,
    route_logits,
):
    ctx_count = lax.axis_size("ctx")
    mp_count = lax.axis_size("mp")
    ctx_index = lax.axis_index("ctx")
    mp_index = lax.axis_index("mp")
    tok_local = queries.shape[0]
    tokens = tok_local * ctx_count
    slot_local = cache_keys.shape[0]
    cache_local = cache_keys.shape[1]
    head_dim = cache_keys.shape[2]
    heads_local = queries.shape[1] // head_dim
    group_size = heads_local // slot_local
    width = cache_local + tok_local
    scale = 1.0 / math.sqrt(head_dim)
    d_local = out_proj.shape[1]
    key_value = jnp.stack(
        [
            jnp.concatenate([cache_keys, new_keys], axis=1),
            jnp.concatenate([cache_values, new_values], axis=1),
        ]
    )
    shaped = queries.reshape(tok_local, slot_local, group_size, head_dim)
    query_block = jnp.transpose(shaped, (1, 2, 0, 3)).reshape(
        slot_local, group_size * tok_local, head_dim
    )
    query_tok = ctx_index * tok_local + jnp.tile(jnp.arange(tok_local, dtype=jnp.int32), group_size)
    query_count = group_size * tok_local
    start_state = (
        jnp.full((slot_local, query_count), neg_big, jnp.float32),
        jnp.zeros((slot_local, query_count), jnp.float32),
        jnp.zeros((slot_local, query_count, head_dim), jnp.float32),
    )
    piece = lax.all_gather(key_value, "ctx", axis=2, tiled=True)
    position = jnp.arange(piece.shape[2], dtype=jnp.int32)
    shard = position // width
    within = position % width
    new_tok = shard * tok_local + within - cache_local
    allowed = (within[None, :] < cache_local) | (new_tok[None, :] <= query_tok[:, None])
    highest, denom, summed = join_softmax(
        start_state, softmax_pieces(query_block, piece[0], piece[1], allowed, scale)
    )
    shaped = (
        (summed / denom[:, :, None])
        .astype(jnp.bfloat16)
        .reshape(slot_local, group_size, tok_local, head_dim)
    )
    attn = jnp.transpose(shaped, (2, 0, 1, 3)).reshape(tok_local, heads_local * head_dim)
    projected = jnp.dot(
        lax.all_gather(attn, "ctx", axis=0, tiled=True),
        out_proj,
        preferred_element_type=jnp.float32,
    )
    res_rows = residual.shape[0]
    res_start = mp_index * res_rows
    current = lax.dynamic_slice_in_dim(projected, res_start, res_rows, 0)
    projected = lax.dynamic_update_slice_in_dim(
        projected, current + residual.astype(jnp.float32), res_start, 0
    )
    hidden = lax.psum(projected.astype(jnp.bfloat16), "mp")
    capacity = tokens * TOP // 4
    slots = route_slots(expert_ids)
    per_row = max(1, EXPERTS // mp_count)
    first_expert = mp_index * EXPERTS // mp_count
    own_expert = (mp_index * ctx_count + ctx_index) * EXPERTS // (ctx_count * mp_count)
    local = own_expert - first_expert
    row_experts = first_expert + jnp.arange(per_row, dtype=jnp.int32)
    match = expert_ids[None, :, :] == row_experts[:, None, None]
    place = jnp.where(match, slots[None, :, :], capacity)
    table = place[:, :, :, None] == jnp.arange(capacity, dtype=jnp.int32)[None, None, None, :]
    pick = jnp.any(table, axis=2)
    packed = jnp.einsum(
        "rtc,td->rcd", pick.astype(jnp.bfloat16), hidden, preferred_element_type=jnp.float32
    ).astype(jnp.bfloat16)
    gate_local = gate_proj[0]
    up_local = up_proj[0]
    down_local = down_proj[0]
    chosen = lax.dynamic_index_in_dim(
        lax.all_gather(packed, "ctx", axis=2, tiled=True), local, 0, keepdims=False
    )
    wide = chosen.astype(jnp.float32)
    gains = norm_gain.astype(jnp.float32)
    scaled = (wide * gains[None, :]).astype(jnp.bfloat16)
    gate_sum = jnp.dot(scaled, gate_local, preferred_element_type=jnp.float32)
    up_sum = jnp.dot(scaled, up_local, preferred_element_type=jnp.float32)
    gate_sum, up_sum, squares = (gate_sum, up_sum, jnp.sum(wide * wide, axis=1))
    rms = lax.rsqrt(squares / D + norm_eps)
    act = (jax.nn.silu(rms[:, None] * gate_sum) * (rms[:, None] * up_sum)).astype(jnp.bfloat16)
    part = lax.dot_general(
        down_local, act, (((0,), (1,)), ((), ())), preferred_element_type=jnp.float32
    )
    returned = lax.psum_scatter(
        jnp.concatenate(
            [jnp.where(local == which, part, 0.0) for which in range(per_row)], axis=1
        ).astype(jnp.bfloat16),
        "ctx",
        scatter_dimension=0,
        tiled=True,
    ).astype(jnp.float32)
    weights = jax.nn.softmax(route_logits, axis=1)
    combine = jnp.sum(jnp.where(table, weights[None, :, :, None], 0.0), axis=2)
    moe = jnp.einsum(
        "drc,rtc->td",
        returned.reshape(d_local, per_row, capacity),
        combine,
        precision=lax.Precision.HIGHEST,
        preferred_element_type=jnp.float32,
    )
    share = lax.psum_scatter(
        moe.astype(jnp.bfloat16), "mp", scatter_dimension=0, tiled=True
    ).astype(jnp.float32)
    own_hidden = lax.dynamic_slice_in_dim(hidden, res_start, res_rows, 0).astype(jnp.float32)
    return (own_hidden + share).astype(jnp.bfloat16)


def solution(mesh):
    placed = (
        P("ctx", "mp"),
        P("mp", "ctx", None),
        P("mp", "ctx", None),
        P("mp", "ctx", None),
        P("mp", "ctx", None),
        P("mp", "ctx"),
        P("mp", "ctx"),
        P(),
        P("ctx", None, "mp"),
        P("ctx", None, "mp"),
        P("ctx", "mp", None),
        P(),
        P(),
    )
    return jax.shard_map(
        on_device, mesh=mesh, in_specs=placed, out_specs=P("mp", "ctx"), check_vma=False
    )
```

profile of v0, /device:TPU:0, one launch (start us, length us, event | category | flops | bytes accessed | tf_op | source)
XLA Modules:
  0.0 234.1 jit_solution(1601538211125830650)
XLA Ops:
  6.5 1.3 maximum_bitcast_fusion
  7.8 0.9 pad_maximum_fusion.1
  8.8 0.8 copy.30
  9.5 0.1 eq.70
  9.7 0.1 eq.66
  9.8 0.6 reduce-window.6
  10.4 0.2 slice_reduce_fusion
  10.7 0.1 fusion.64
  10.8 0.1 broadcast_in_dim.67
  11.0 0.1 add.99
  11.1 0.1 reshape.149
  11.3 0.3 compare_or_fusion
  11.6 37.6 %all-gather.3.cloned.1.call-done = bf16[2,2,4224,128]{3,2,1,0:T(8,128)(2,1)} async-done(((bf16[2,2,528,128]{3,2,1,0:T(8,128)(2,1)}), bf16[2,2,4224,128]{3,2,1,0:T(8,128)(2,1)}) %all-gather.3.cloned.1.call-update) | async-done | bytes 4325392 | tf_op jit(solution)/shard_map/all_gather | solution.py:90
  49.3 2.8 %fusion.74 = (f32[2,96]{1,0:T(2,128)S(1)}, f32[2,96,4224]{2,1,0:T(8,128)S(1)}) fusion(bf16[2,96,128]{2,1,0:T(8,128)(2,1)S(1)} %bitcast.87, bf16[2,2,4224,128]{3,2,1,0:T(8,128)(2,1)} %all-gather.3.cloned.1.call-done, pred[96,4224]{1,0:T(8,128)(4,1)S(1)} %compare_or_fusion), kind=kOutput, calls=%fused_computation.88 | convolution fusion | flops 210050880 | bytes 5862144 | tf_op jit(solution)/shard_map/srd,skd->srk/dot_general | solution.py:23
  52.1 0.6 fusion.8
  52.7 0.8 fusion.36
  53.6 0.1 reshape.152
  53.7 9.6 %all_gather.10 = bf16[128,1536]{1,0:T(8,128)(2,1)S(1)} all-gather(bf16[16,1536]{1,0:T(8,128)(2,1)S(1)} %reshape.152), channel_id=1, replica_groups=mesh['ctx'=8,'mp'=4] {'ctx'}, dimensions={0}, use_global_device_ids=true | all-gather | bytes 442368 | tf_op jit(solution)/shard_map/all_gather | solution.py:106
  63.2 0.5 fusion.81
  63.7 0.7 convert_element_type.59
  64.6 34.8 %all-reduce.2.cloned.1.call-done = bf16[128,768]{1,0:T(8,128)(2,1)} async-done(((bf16[128,768]{1,0:T(8,128)(2,1)}), bf16[128,768]{1,0:T(8,128)(2,1)}) %all-reduce.2.cloned.1.call-update) | async-done | bytes 196624 | tf_op jit(solution)/shard_map/psum | solution.py:116
  99.5 1.8 convolution_convert_fusion
  101.3 0.2 reduce-scatter.3.cloned.1.call-start
  101.6 25.4 %all-gather.5.cloned.1.call-done = bf16[2,64,6144]{2,1,0:T(8,128)(2,1)} async-done(((bf16[2,64,768]{2,1,0:T(8,128)(2,1)}), bf16[2,64,6144]{2,1,0:T(8,128)(2,1)}) %all-gather.5.cloned.1.call-update) | async-done | bytes 1572880 | tf_op jit(solution)/shard_map/all_gather | solution.py:135
  127.0 1.4 fusion.27
  128.4 13.7 %fusion.10 = f32[64,2048]{1,0:T(8,128)} fusion(bf16[1,6144,2048]{2,1,0:T(8,128)(2,1)} %param.21, f32[6144]{0:T(1024)S(1)} %convert_element_type.65, bf16[2,64,6144]{2,1,0:T(8,128)(2,1)} %all-gather.5.cloned.1.call-done, s32[]{:T(128)S(6)} %select_n.86, f32[64]{0:T(128)S(1)} %add_rsqrt_fusion), kind=kOutput, calls=%fused_computation.12 | convolution fusion | flops 1611923456 | bytes 26501380 | tf_op jit(solution)/shard_map/dot_general | solution.py:140
  142.1 21.4 %fusion.39 = (bf16[6144,64]{0,1:T(8,128)(2,1)S(1)}, bf16[6144,64]{0,1:T(8,128)(2,1)}) fusion(pred[]{:T(512)S(6)} %eq.77, pred[]{:T(512)S(6)} %eq.78, bf16[1,2048,6144]{2,1,0:T(8,128)(2,1)} %param.23, bf16[1,6144,2048]{2,1,0:T(8,128)(2,1)} %param.22, f32[6144]{0:T(1024)S(1)} %convert_element_type.65, bf16[2,64,6144]{2,1,0:T(8,128)(2,1)} %all-gather.5.cloned.1.call-done, ...), kind=kOutput, calls=%fused_computation.34 | convolution fusion | flops 3224109056 | bytes 53240072 | tf_op jit(solution)/shard_map/dot_general | solution.py:145
  163.5 2.4 %pad_maximum_fusion = bf16[6144,128]{0,1:T(8,128)(2,1)} fusion(bf16[6144,64]{0,1:T(8,128)(2,1)} %get-tuple-element.6, bf16[6144,64]{0,1:T(8,128)(2,1)S(1)} %get-tuple-element.5), kind=kLoop, calls=%fused_computation.25 | loop fusion | flops 3145728 | bytes 3145728 | tf_op jit(solution)/shard_map/concatenate | solution.py:149
  166.1 38.5 %reduce-scatter.3.cloned.1.call-done = bf16[768,128]{0,1:T(8,128)(2,1)} async-done(((bf16[6144,128]{0,1:T(8,128)(2,1)}), bf16[768,128]{0,1:T(8,128)(2,1)}) %reduce-scatter.3.cloned.1.call-update) | async-done | bytes 196624 | tf_op jit(solution)/shard_map/reduce_scatter | solution.py:148
  204.6 2.0 fusion.29
  206.6 19.6 %reduce-scatter.5.cloned.1.call-done = bf16[32,768]{1,0:T(8,128)(2,1)} async-done(((bf16[128,768]{1,0:T(8,128)(2,1)}), bf16[32,768]{1,0:T(8,128)(2,1)}) %reduce-scatter.5.cloned.1.call-update) | async-done | bytes 49168 | tf_op jit(solution)/shard_map/reduce_scatter | solution.py:165
  226.1 1.5 add_convert_fusion
  (48 shorter events, 0.6 us)
Async XLA Ops:
  6.5 56.7 %copy-start = (bf16[1536,768]{1,0:T(8,128)(2,1)S(1)}, bf16[1536,768]{1,0:T(8,128)(2,1)}, u32[]{:S(2)}) copy-start(bf16[1536,768]{1,0:T(8,128)(2,1)} %param.18) | copy-start | bytes 7077892
  6.5 4.6 %copy-start.2 = (bf16[16,1536]{1,0:T(8,128)(2,1)S(1)}, bf16[16,1536]{1,0:T(8,128)(2,1)}, u32[]{:S(2)}) copy-start(bf16[16,1536]{1,0:T(8,128)(2,1)} %param.13) | copy-start | bytes 147460
  6.5 42.7 %all-gather.3.cloned.1.call-start = ((), (), s32[]{:S(2)}) async-start(), calls=%async_computation.2 | async-start | bytes 4866048 | tf_op jit(solution)/shard_map/all_gather | solution.py:90
  8.7 90.8 %all-reduce.2.cloned.1.call-start = ((), (), s32[]{:S(2)}) async-start(), calls=%async_computation.3 | async-start | bytes 393216 | tf_op jit(solution)/shard_map/psum | solution.py:116
  49.3 3.4 %slice-start = ((s8[4325376]{0:T(1024)(128)(4,1)}), s8[4194304]{0:T(1024)(128)(4,1)S(1)}, s32[]{:S(2)}) async-start(s8[4325376]{0:T(1024)(128)(4,1)} %bitcast.89), calls=%async_computation.7 | async-start | bytes 8388608
  49.3 3.4 %slice-start.1 = ((s8[4325376]{0:T(1024)(128)(4,1)}), s8[131072]{0:T(1024)(128)(4,1)S(1)}, s32[]{:S(2)}) async-start(s8[4325376]{0:T(1024)(128)(4,1)} %bitcast.89), calls=%async_computation.8 | async-start | bytes 262144
  53.5 10.2 %copy-start.3 = (bf16[32,768]{1,0:T(8,128)(2,1)S(1)}, bf16[32,768]{1,0:T(8,128)(2,1)}, u32[]{:S(2)}) copy-start(bf16[32,768]{1,0:T(8,128)(2,1)} %param.19) | copy-start | bytes 147460
  53.5 11.0 %copy-start.6 = (s32[128,2]{0,1:T(2,128)S(1)}, s32[128,2]{0,1:T(2,128)}, u32[]{:S(2)}) copy-start(s32[128,2]{0,1:T(2,128)} %param.24) | copy-start | bytes 3076
  53.5 48.0 %copy-start.4 = (bf16[6144]{0:T(1024)(128)(2,1)S(1)}, bf16[6144]{0:T(1024)(128)(2,1)}, u32[]{:S(2)}) copy-start(bf16[6144]{0:T(1024)(128)(2,1)} %param.20) | copy-start | bytes 36868
  64.4 62.5 %all-gather.5.cloned.1.call-start = ((), (), s32[]{:S(2)}) async-start(), calls=%async_computation.4 | async-start | bytes 1769472 | tf_op jit(solution)/shard_map/all_gather | solution.py:135
  101.3 103.3 %reduce-scatter.3.cloned.1.call-start = ((), (), s32[]{:S(2)}) async-start(), calls=%async_computation.5 | async-start | bytes 1769472 | tf_op jit(solution)/shard_map/reduce_scatter | solution.py:148
  142.1 85.5 %copy-start.1 = (bf16[1536,768]{1,0:T(8,128)(2,1)S(1)}, bf16[1536,768]{1,0:T(8,128)(2,1)}, u32[]{:S(2)}) copy-start(bf16[1536,768]{1,0:T(8,128)(2,1)} %param.18) | copy-start | bytes 7077892
  163.5 2.5 %copy-start.5 = (f32[128,2]{0,1:T(2,128)S(1)}, f32[128,2]{0,1:T(2,128)}, u32[]{:S(2)}) copy-start(f32[128,2]{0,1:T(2,128)} %param.25) | copy-start | bytes 3076
  166.0 60.2 %reduce-scatter.5.cloned.1.call-start = ((), (), s32[]{:S(2)}) async-start(), calls=%async_computation.6 | async-start | bytes 245760 | tf_op jit(solution)/shard_map/reduce_scatter | solution.py:165
Sparse Core Ops, SparseCore 0:
  9.3 39.9 all-gather.2
  64.6 34.8 all-reduce.1
  101.5 25.3 all-gather.4
  166.1 38.4 reduce-scatter.2
  206.8 19.3 reduce-scatter.4
where the time goes:
time: 235 us; the launch traced here: 234 us
  waiting for transfers between devices  156 us (66%)
  matrix products  42.9 us (18%)
  between operations  13.4 us (6%)
  other arithmetic  10 us (4%)
  blocking collectives  9.55 us (4%)
    reduce_scatter x1, waiting for transfers between devices, on_device(): lax.psum_scatter(jnp.concatenate([jnp.where(local == which, part, 0.0) fo...  38.5 us
    all_gather x1, waiting for transfers between devices, on_device(): piece = lax.all_gather(key_value, 'ctx', axis=2, tiled=True)  37.6 us
    psum x1, waiting for transfers between devices, on_device(): hidden = lax.psum(projected.astype(jnp.bfloat16), 'mp')  34.8 us
    all_gather x1, waiting for transfers between devices, on_device(): lax.all_gather(packed, 'ctx', axis=2, tiled=True)  25.4 us
    dot_general x1, matrix products, on_device(): lax.dot_general(down_local, act, (((0,), (1,)), ((), ())), preferred_elem...  21.4 us
    reduce_scatter x1, waiting for transfers between devices, on_device(): lax.psum_scatter(moe.astype(jnp.bfloat16), 'mp', scatter_dimension=0, til...  19.6 us
    dot_general x1, matrix products, on_device(): gate_sum = jnp.dot(scaled, gate_local, preferred_element_type=jnp.float32)  13.7 us
    all_gather x1, blocking collectives, on_device(): lax.all_gather(attn, 'ctx', axis=0, tiled=True)  9.55 us
  transfers between devices with their start and end apart: 5, of which 5 were waited for; matrix products, arithmetic and copies ran while one was open for 1% of the time, Pallas kernels for 0%

commit v1 on v0

--- a/solution.py
+++ b/solution.py
@@ -3,6 +3,7 @@
 import jax.numpy as jnp
 from jax import lax
 from jax.sharding import PartitionSpec as P
+from jax.lax import axis_index, axis_size, ppermute
 
 D = 6144
 EXPERTS = 8
@@ -87,7 +88,16 @@
         jnp.zeros((slot_local, query_count), jnp.float32),
         jnp.zeros((slot_local, query_count, head_dim), jnp.float32),
     )
-    piece = lax.all_gather(key_value, "ctx", axis=2, tiled=True)
+    num_devices = axis_size("ctx")
+    all_blocks = [(u, (u + 1) % num_devices) for u in range(num_devices)]
+    copies = [(u, (u - 1) % num_devices) for u in range(num_devices)]
+    upper, f_now = ([key_value], [key_value])
+    for _ in range(num_devices // 2):
+        upper.append(ppermute(upper[-1], "ctx", all_blocks))
+    for _ in [*range((num_devices - 1) // 2)]:
+        f_now.append(ppermute(f_now[-1], "ctx", copies))
+    main = jnp.concatenate([*upper[::-1], *f_now[1:]], axis=2)
+    piece = jnp.roll(main, (axis_index("ctx") - num_devices // 2) * key_value.shape[2], 2)
     position = jnp.arange(piece.shape[2], dtype=jnp.int32)
     shard = position // width
     within = position % width

time: 235 us -> 263 us (1.12)
  local copies, waits for them, and re-layouts: 1.81 us -> 15.1 us
  starting transfers between devices: 0.35 us -> 8.91 us
  blocking collectives: 9.55 us -> 15.1 us
    ppermute x0 -> x7, waiting for transfers between devices: none -> 39.3 us  [the longest x4 39.1 us: on_device(): upper.append(ppermute(upper[-1], 'ctx', all_blocks))]
    all_gather x1 -> x0, waiting for transfers between devices: 37.6 us -> none  [on_device(): piece = lax.all_gather(key_value, 'ctx', axis=2, tiled=True)]
    unnamed x19 -> x30, local copies, waits for them, and re-layouts: 0.83 us -> 13.2 us
    ppermute x0 -> x7, starting transfers between devices: none -> 8.6 us  [the longest x3 8.14 us: on_device(): f_now.append(ppermute(f_now[-1], 'ctx', copies))]
    all_gather x1, blocking collectives: 9.55 us -> 15.1 us  [on_device(): lax.all_gather(attn, 'ctx', axis=0, tiled=True)]
  transfers between devices with their start and end apart: 5 -> 11, of which waited for: 5 -> 9; matrix products, arithmetic and copies ran while one was open for 1% -> 4% of each run, Pallas kernels for 0% -> 0%
where the time goes in v1:
time: 263 us; the launch traced here: 262 us
  waiting for transfers between devices  158 us (60%)
  matrix products  42 us (16%)
  local copies, waits for them, and re-layouts  15.1 us (6%)
  blocking collectives  15.1 us (6%)
  between operations  13.5 us (5%)
  other arithmetic  10.1 us (4%)
  starting transfers between devices  8.91 us (3%)
    ppermute x4, waiting for transfers between devices, on_device(): upper.append(ppermute(upper[-1], 'ctx', all_blocks))  39.1 us
    reduce_scatter x1, waiting for transfers between devices, on_device(): lax.psum_scatter(jnp.concatenate([jnp.where(local == which, part, 0.0) fo...  38.5 us
    psum x1, waiting for transfers between devices, on_device(): hidden = lax.psum(projected.astype(jnp.bfloat16), 'mp')  34.9 us
    all_gather x1, waiting for transfers between devices, on_device(): lax.all_gather(packed, 'ctx', axis=2, tiled=True)  25.4 us
    dot_general x1, matrix products, on_device(): lax.dot_general(down_local, act, (((0,), (1,)), ((), ())), preferred_elem...  21.4 us
    reduce_scatter x1, waiting for transfers between devices, on_device(): lax.psum_scatter(moe.astype(jnp.bfloat16), 'mp', scatter_dimension=0, til...  19.6 us
    all_gather x1, blocking collectives, on_device(): lax.all_gather(attn, 'ctx', axis=0, tiled=True)  15.1 us
    dot_general x1, matrix products, on_device(): gate_sum = jnp.dot(scaled, gate_local, preferred_element_type=jnp.float32)  13.7 us
  transfers between devices with their start and end apart: 11, of which 9 were waited for; matrix products, arithmetic and copies ran while one was open for 4% of the time, Pallas kernels for 0%

profile of v1, /device:TPU:0, one launch (start us, length us, event | category | flops | bytes accessed | tf_op | source)
XLA Modules:
  0.0 262.4 jit_solution(7812944390052913208)
XLA Ops:
  6.5 1.2 maximum_bitcast_fusion
  9.1 10.1 %collective-permute-done = bf16[2,2,528,128]{3,2,1,0:T(8,128)(2,1)S(1)} collective-permute-done((bf16[2,2,528,128]{3,2,1,0:T(8,128)(2,1)}, bf16[2,2,528,128]{3,2,1,0:T(8,128)(2,1)S(1)}, u32[]{:S(2)}, u32[]{:S(2)}) %collective-permute-start) | collective-permute-done | bytes 540704 | tf_op jit(solution)/shard_map/ppermute | solution.py:96
  19.2 2.6 %collective-permute-start.4 = (bf16[2,2,528,128]{3,2,1,0:T(8,128)(2,1)}, bf16[2,2,528,128]{3,2,1,0:T(8,128)(2,1)}, u32[]{:S(2)}, u32[]{:S(2)}) collective-permute-start(bf16[2,2,528,128]{3,2,1,0:T(8,128)(2,1)} %pad_maximum_fusion.1), channel_id=1, source_target_pairs={{0,28},{4,0},{8,4},{12,8},{16,12},{20,16},{24,20},{28,24},{1,29},{... | collective-permute-start | bytes 1622024 | tf_op jit(solution)/shard_map/ppermute | solution.py:98
  22.0 10.8 %collective-permute-done.1 = bf16[2,2,528,128]{3,2,1,0:T(8,128)(2,1)} collective-permute-done((bf16[2,2,528,128]{3,2,1,0:T(8,128)(2,1)S(1)}, bf16[2,2,528,128]{3,2,1,0:T(8,128)(2,1)}, u32[]{:S(2)}, u32[]{:S(2)}) %collective-permute-start.1) | collective-permute-done | bytes 540704 | tf_op jit(solution)/shard_map/ppermute | solution.py:96
  35.2 2.7 %collective-permute-start.5 = (bf16[2,2,528,128]{3,2,1,0:T(8,128)(2,1)}, bf16[2,2,528,128]{3,2,1,0:T(8,128)(2,1)}, u32[]{:S(2)}, u32[]{:S(2)}) collective-permute-start(bf16[2,2,528,128]{3,2,1,0:T(8,128)(2,1)} %collective-permute-done.4), channel_id=1, source_target_pairs={{0,28},{4,0},{8,4},{12,8},{16,12},{20,16},{24,20},{28,24},{1,29},{... | collective-permute-start | bytes 1622024 | tf_op jit(solution)/shard_map/ppermute | solution.py:98
  37.9 8.4 %collective-permute-done.2 = bf16[2,2,528,128]{3,2,1,0:T(8,128)(2,1)} collective-permute-done((bf16[2,2,528,128]{3,2,1,0:T(8,128)(2,1)}, bf16[2,2,528,128]{3,2,1,0:T(8,128)(2,1)}, u32[]{:S(2)}, u32[]{:S(2)}) %collective-permute-start.2) | collective-permute-done | bytes 540704 | tf_op jit(solution)/shard_map/ppermute | solution.py:96
  47.6 2.8 %collective-permute-start.6 = (bf16[2,2,528,128]{3,2,1,0:T(8,128)(2,1)}, bf16[2,2,528,128]{3,2,1,0:T(8,128)(2,1)S(1)}, u32[]{:S(2)}, u32[]{:S(2)}) collective-permute-start(bf16[2,2,528,128]{3,2,1,0:T(8,128)(2,1)} %collective-permute-done.5), channel_id=1, source_target_pairs={{0,28},{4,0},{8,4},{12,8},{16,12},{20,16},{24,20},{28,24},{1,29},{... | collective-permute-start | bytes 1622024 | tf_op jit(solution)/shard_map/ppermute | solution.py:98
  50.4 9.8 %collective-permute-done.3 = bf16[2,2,528,128]{3,2,1,0:T(8,128)(2,1)} collective-permute-done((bf16[2,2,528,128]{3,2,1,0:T(8,128)(2,1)}, bf16[2,2,528,128]{3,2,1,0:T(8,128)(2,1)}, u32[]{:S(2)}, u32[]{:S(2)}) %collective-permute-start.3) | collective-permute-done | bytes 540704 | tf_op jit(solution)/shard_map/ppermute | solution.py:96
  61.3 1.1 constant_dynamic-update-slice_fusion.14
  62.4 1.1 constant_dynamic-update-slice_fusion.13
  63.5 1.1 constant_dynamic-update-slice_fusion.12
  64.8 1.1 constant_dynamic-update-slice_fusion.10
  65.9 1.1 constant_dynamic-update-slice_fusion.9
  67.1 1.1 constant_dynamic-update-slice_fusion.7
  68.2 1.1 constant_dynamic-update-slice_fusion.6
  69.3 1.1 constant_dynamic-update-slice_fusion.5
  70.6 1.1 constant_dynamic-update-slice_fusion.2
  71.7 1.1 constant_dynamic-update-slice_fusion.1
  73.0 1.5 fusion.76
  75.1 1.2 fusion.36
  76.4 15.1 %all_gather.6 = bf16[128,1536]{1,0:T(8,128)(2,1)S(1)} all-gather(bf16[16,1536]{1,0:T(8,128)(2,1)S(1)} %reshape.152), channel_id=1, replica_groups=mesh['ctx'=8,'mp'=4] {'ctx'}, dimensions={0}, use_global_device_ids=true | all-gather | bytes 442368 | tf_op jit(solution)/shard_map/all_gather | solution.py:116
  92.9 34.9 %all-reduce.2.cloned.1.call-done = bf16[128,768]{1,0:T(8,128)(2,1)} async-done(((bf16[128,768]{1,0:T(8,128)(2,1)}), bf16[128,768]{1,0:T(8,128)(2,1)}) %all-reduce.2.cloned.1.call-update) | async-done | bytes 196624 | tf_op jit(solution)/shard_map/psum | solution.py:126
  127.8 1.8 convolution_convert_fusion
  129.9 25.4 %all-gather.2.cloned.1.call-done = bf16[2,64,6144]{2,1,0:T(8,128)(2,1)} async-done(((bf16[2,64,768]{2,1,0:T(8,128)(2,1)}), bf16[2,64,6144]{2,1,0:T(8,128)(2,1)}) %all-gather.2.cloned.1.call-update) | async-done | bytes 1572880 | tf_op jit(solution)/shard_map/all_gather | solution.py:145
  155.3 1.4 fusion.27
  156.7 13.7 %fusion.10 = f32[64,2048]{1,0:T(8,128)} fusion(bf16[1,6144,2048]{2,1,0:T(8,128)(2,1)} %param.21, f32[6144]{0:T(1024)S(1)} %convert_element_type.65, bf16[2,64,6144]{2,1,0:T(8,128)(2,1)} %all-gather.2.cloned.1.call-done, s32[]{:T(128)S(6)} %select_n.100, f32[64]{0:T(128)S(1)} %add_rsqrt_fusion), kind=kOutput, calls=%fused_computation.12 | convolution fusion | flops 1611923456 | bytes 26501380 | tf_op jit(solution)/shard_map/dot_general | solution.py:150
  170.4 21.4 %fusion.39 = (bf16[6144,64]{0,1:T(8,128)(2,1)S(1)}, bf16[6144,64]{0,1:T(8,128)(2,1)}) fusion(pred[]{:T(512)S(6)} %eq.80, pred[]{:T(512)S(6)} %eq.81, bf16[1,2048,6144]{2,1,0:T(8,128)(2,1)} %param.23, bf16[1,6144,2048]{2,1,0:T(8,128)(2,1)} %param.22, f32[6144]{0:T(1024)S(1)} %convert_element_type.65, bf16[2,64,6144]{2,1,0:T(8,128)(2,1)} %all-gather.2.cloned.1.call-done, ...), kind=kOutput, calls=%fused_computation.34 | convolution fusion | flops 3224109056 | bytes 53240072 | tf_op jit(solution)/shard_map/dot_general | solution.py:155
  191.8 2.4 pad_maximum_fusion
  194.4 38.5 %reduce-scatter.3.cloned.1.call-done = bf16[768,128]{0,1:T(8,128)(2,1)} async-done(((bf16[6144,128]{0,1:T(8,128)(2,1)}), bf16[768,128]{0,1:T(8,128)(2,1)}) %reduce-scatter.3.cloned.1.call-update) | async-done | bytes 196624 | tf_op jit(solution)/shard_map/reduce_scatter | solution.py:158
  232.9 2.0 fusion.29
  234.9 19.6 %reduce-scatter.5.cloned.1.call-done = bf16[32,768]{1,0:T(8,128)(2,1)} async-done(((bf16[128,768]{1,0:T(8,128)(2,1)}), bf16[32,768]{1,0:T(8,128)(2,1)}) %reduce-scatter.5.cloned.1.call-update) | async-done | bytes 49168 | tf_op jit(solution)/shard_map/reduce_scatter | solution.py:175
  254.5 1.5 add_convert_fusion
  (72 shorter events, 8.9 us)
Async XLA Ops:
  6.5 85.0 %copy-start = (bf16[1536,768]{1,0:T(8,128)(2,1)S(1)}, bf16[1536,768]{1,0:T(8,128)(2,1)}, u32[]{:S(2)}) copy-start(bf16[1536,768]{1,0:T(8,128)(2,1)} %param.18) | copy-start | bytes 7077892
  6.5 121.2 %all-reduce.2.cloned.1.call-start = ((), (), s32[]{:S(2)}) async-start(), calls=%async_computation.2 | async-start | bytes 393216 | tf_op jit(solution)/shard_map/psum | solution.py:126
  8.6 10.6 %collective-permute-start = (bf16[2,2,528,128]{3,2,1,0:T(8,128)(2,1)}, bf16[2,2,528,128]{3,2,1,0:T(8,128)(2,1)S(1)}, u32[]{:S(2)}, u32[]{:S(2)}) collective-permute-start(bf16[2,2,528,128]{3,2,1,0:T(8,128)(2,1)} %pad_maximum_fusion.1), channel_id=1, source_target_pairs={{0,4},{4,8},{8,12},{12,16},{16,20},{20,24},{24,28},{28,0},{1,5},{5... | collective-permute-start | bytes 1622024 | tf_op jit(solution)/shard_map/ppermute | solution.py:96
  19.2 13.6 %copy-start.2 = (bf16[2,2,528,128]{3,2,1,0:T(8,128)(2,1)}, bf16[2,2,528,128]{3,2,1,0:T(8,128)(2,1)S(1)}, u32[]{:S(2)}) copy-start(bf16[2,2,528,128]{3,2,1,0:T(8,128)(2,1)S(1)} %collective-permute-done) | copy-start | bytes 1622020
  19.2 13.6 %collective-permute-start.1 = (bf16[2,2,528,128]{3,2,1,0:T(8,128)(2,1)S(1)}, bf16[2,2,528,128]{3,2,1,0:T(8,128)(2,1)}, u32[]{:S(2)}, u32[]{:S(2)}) collective-permute-start(bf16[2,2,528,128]{3,2,1,0:T(8,128)(2,1)S(1)} %collective-permute-done), channel_id=1, source_target_pairs={{0,4},{4,8},{8,12},{12,16},{16,20},{20,24},{24,28},{28,0},{1,5},{5... | collective-permute-start | bytes 1622024 | tf_op jit(solution)/shard_map/ppermute | solution.py:96
  19.2 16.0 %collective-permute-start.4 = (bf16[2,2,528,128]{3,2,1,0:T(8,128)(2,1)}, bf16[2,2,528,128]{3,2,1,0:T(8,128)(2,1)}, u32[]{:S(2)}, u32[]{:S(2)}) collective-permute-start(bf16[2,2,528,128]{3,2,1,0:T(8,128)(2,1)} %pad_maximum_fusion.1), channel_id=1, source_target_pairs={{0,28},{4,0},{8,4},{12,8},{16,12},{20,16},{24,20},{28,24},{1,29},{... | collective-permute-start | bytes 1622024 | tf_op jit(solution)/shard_map/ppermute | solution.py:98
  32.8 13.4 %collective-permute-start.2 = (bf16[2,2,528,128]{3,2,1,0:T(8,128)(2,1)}, bf16[2,2,528,128]{3,2,1,0:T(8,128)(2,1)}, u32[]{:S(2)}, u32[]{:S(2)}) collective-permute-start(bf16[2,2,528,128]{3,2,1,0:T(8,128)(2,1)} %collective-permute-done.1), channel_id=1, source_target_pairs={{0,4},{4,8},{8,12},{12,16},{16,20},{20,24},{24,28},{28,0},{1,5},{5... | collective-permute-start | bytes 1622024 | tf_op jit(solution)/shard_map/ppermute | solution.py:96
  35.2 12.4 %collective-permute-start.5 = (bf16[2,2,528,128]{3,2,1,0:T(8,128)(2,1)}, bf16[2,2,528,128]{3,2,1,0:T(8,128)(2,1)}, u32[]{:S(2)}, u32[]{:S(2)}) collective-permute-start(bf16[2,2,528,128]{3,2,1,0:T(8,128)(2,1)} %collective-permute-done.4), channel_id=1, source_target_pairs={{0,28},{4,0},{8,4},{12,8},{16,12},{20,16},{24,20},{28,24},{1,29},{... | collective-permute-start | bytes 1622024 | tf_op jit(solution)/shard_map/ppermute | solution.py:98
  46.3 14.0 %collective-permute-start.3 = (bf16[2,2,528,128]{3,2,1,0:T(8,128)(2,1)}, bf16[2,2,528,128]{3,2,1,0:T(8,128)(2,1)}, u32[]{:S(2)}, u32[]{:S(2)}) collective-permute-start(bf16[2,2,528,128]{3,2,1,0:T(8,128)(2,1)} %collective-permute-done.2), channel_id=1, source_target_pairs={{0,4},{4,8},{8,12},{12,16},{16,20},{20,24},{24,28},{28,0},{1,5},{5... | collective-permute-start | bytes 1622024 | tf_op jit(solution)/shard_map/ppermute | solution.py:96
  47.4 23.0 %copy-start.3 = (bf16[2,2,528,128]{3,2,1,0:T(8,128)(2,1)S(1)}, bf16[2,2,528,128]{3,2,1,0:T(8,128)(2,1)}, u32[]{:S(2)}) copy-start(bf16[2,2,528,128]{3,2,1,0:T(8,128)(2,1)} %copy-done.2) | copy-start | bytes 1622020
  47.6 19.4 %collective-permute-start.6 = (bf16[2,2,528,128]{3,2,1,0:T(8,128)(2,1)}, bf16[2,2,528,128]{3,2,1,0:T(8,128)(2,1)S(1)}, u32[]{:S(2)}, u32[]{:S(2)}) collective-permute-start(bf16[2,2,528,128]{3,2,1,0:T(8,128)(2,1)} %collective-permute-done.5), channel_id=1, source_target_pairs={{0,28},{4,0},{8,4},{12,8},{16,12},{20,16},{24,20},{28,24},{1,29},{... | collective-permute-start | bytes 1622024 | tf_op jit(solution)/shard_map/ppermute | solution.py:98
  72.9 19.1 %copy-start.4 = (bf16[32,768]{1,0:T(8,128)(2,1)S(1)}, bf16[32,768]{1,0:T(8,128)(2,1)}, u32[]{:S(2)}) copy-start(bf16[32,768]{1,0:T(8,128)(2,1)} %param.19) | copy-start | bytes 147460
  73.0 19.9 %copy-start.7 = (s32[128,2]{0,1:T(2,128)S(1)}, s32[128,2]{0,1:T(2,128)}, u32[]{:S(2)}) copy-start(s32[128,2]{0,1:T(2,128)} %param.24) | copy-start | bytes 3076
  74.5 55.4 %copy-start.5 = (bf16[6144]{0:T(1024)(128)(2,1)S(1)}, bf16[6144]{0:T(1024)(128)(2,1)}, u32[]{:S(2)}) copy-start(bf16[6144]{0:T(1024)(128)(2,1)} %param.20) | copy-start | bytes 36868
  92.8 62.5 %all-gather.2.cloned.1.call-start = ((), (), s32[]{:S(2)}) async-start(), calls=%async_computation.3 | async-start | bytes 1769472 | tf_op jit(solution)/shard_map/all_gather | solution.py:145
  129.6 103.3 %reduce-scatter.3.cloned.1.call-start = ((), (), s32[]{:S(2)}) async-start(), calls=%async_computation.4 | async-start | bytes 1769472 | tf_op jit(solution)/shard_map/reduce_scatter | solution.py:158
  170.4 23.9 %copy-start.6 = (f32[128,2]{0,1:T(2,128)S(1)}, f32[128,2]{0,1:T(2,128)}, u32[]{:S(2)}) copy-start(f32[128,2]{0,1:T(2,128)} %param.25) | copy-start | bytes 3076
  170.4 85.5 %copy-start.1 = (bf16[1536,768]{1,0:T(8,128)(2,1)S(1)}, bf16[1536,768]{1,0:T(8,128)(2,1)}, u32[]{:S(2)}) copy-start(bf16[1536,768]{1,0:T(8,128)(2,1)} %param.18) | copy-start | bytes 7077892
  194.3 60.2 %reduce-scatter.5.cloned.1.call-start = ((), (), s32[]{:S(2)}) async-start(), calls=%async_computation.5 | async-start | bytes 245760 | tf_op jit(solution)/shard_map/reduce_scatter | solution.py:175
Sparse Core Ops, SparseCore 0:
  92.9 34.8 all-reduce.1
  129.8 25.3 all-gather.1
  194.4 38.4 reduce-scatter.2
  235.1 19.3 reduce-scatter.4
